TPU v7x, 32 devices: a whole 2x2x4 slice. The times are simulated.
32 devices in a mesh: rep: 2 (over x), walk: 16 (over z, y, core).
Axes of the slice: x: 2, y: 2, z: 4, core: 2. Of those that a mesh axis runs over, the one named last changes fastest.
Arguments:
- greens: bfloat16 [32, 64, 384], P(('rep', 'walk')), parts along dimension 0, may hold values from -6 to 6
- source: int32 [64], P(('rep', 'walk')), parts along dimension 0, may hold values from 0 to 15, as said below
- counts: int32 [32], P('rep'), parts along dimension 0, may hold values from 1 to 2, as said below
- cholesky: bfloat16 [512, 64, 384], P('walk'), may hold values from -0.0390625 to 0.0390625
Outputs:
- relocated: bfloat16 [64, 64, 384], P(('rep', 'walk')), parts along dimension 0
- exchange_energy: float32 [64], P(('rep', 'walk')), parts along dimension 0
- force_bias: float32 [64, 512], P(('rep', 'walk')), parts along dimension 0
There are 2 independent parts, one for each index of `rep`. A program takes and returns all parts, laid end to end along the dimension named above; an argument that names none is the same for every part. Nothing has to cross between parts.
Inputs may be any that keep to these rules, and one draw needn't show every extreme that they name: `source`: slot s belongs to walk device s div 2. Its walker comes from that device or one of the two devices beside it along the closed loop of walk devices. Slots beyond a device's count also name some walker. Slots 0 to counts[d] - 1 of device d are live.
All inputs are finite; a program needn't handle non-finite values.
Results may differ from a plain program's by a relative error of at most 0.001.
Values may be sent and summed in bfloat16 or wider, within the bound.
A program may use at most 64 MiB of HBM per device.

v0:
```python
import jax
import jax.numpy as jnp
from jax import lax
from jax.sharding import PartitionSpec as P


def padded(block, sides, width):
    for axis, dim in sides:
        count = lax.axis_size(axis)
        forward = [(i, i + 1) for i in range(count - 1)]
        forward.append((count - 1, 0))
        backward = [(target, source) for source, target in forward]
        low = lax.ppermute(
            lax.slice_in_dim(block, block.shape[dim] - width, None, axis=dim), axis, forward
        )
        high = lax.ppermute(lax.slice_in_dim(block, 0, width, axis=dim), axis, backward)
        block = jnp.concatenate([low, block, high], axis=dim)
    return block


def body(greens, source, counts, cholesky):
    walkers = lax.axis_size("walk")
    my_index = lax.axis_index("walk")
    old_slots = greens.shape[0]
    new_slots = source.shape[0]
    chol_dev = cholesky.shape[0]
    occupied = cholesky.shape[1]
    orbitals = cholesky.shape[2]
    nchol = chol_dev * walkers
    nearby = padded(greens, (("walk", 0),), old_slots)
    src_dev = source // old_slots
    relative = (src_dev - my_index + 1) % walkers
    chosen = relative * old_slots + source % old_slots
    my_count = lax.dynamic_index_in_dim(counts, my_index, 0, keepdims=False)
    is_live = jnp.arange(new_slots) < my_count
    relocated = jnp.where(
        is_live[:, None, None], jnp.take(nearby, chosen, axis=0), jnp.zeros((), jnp.bfloat16)
    )
    chol_rows = cholesky.reshape(chol_dev, occupied * orbitals)
    batch_dims = (((2,), (2,)), ((0,), (0,)))

    def group_energy(group_in):
        members = group_in.shape[0]
        spread = jnp.broadcast_to(
            group_in[:, None], (members, chol_dev, occupied, orbitals)
        ).reshape(members * chol_dev, occupied, orbitals)
        stacked = jnp.broadcast_to(cholesky[None], (members, chol_dev, occupied, orbitals)).reshape(
            members * chol_dev, occupied, orbitals
        )
        forward = lax.dot_general(stacked, spread, batch_dims, preferred_element_type=jnp.float32)
        mirrored = lax.dot_general(spread, stacked, batch_dims, preferred_element_type=jnp.float32)
        return -(0.5 / nchol) * jnp.sum((forward * mirrored).reshape(members, -1), axis=1)

    block_in = lax.all_gather(greens, "walk", axis=0, tiled=True)
    total_rows = block_in.shape[0]
    group = 1
    for candidate in range(1, 5):
        if total_rows % candidate == 0:
            group = candidate
    grouped = block_in.reshape(total_rows // group, group, occupied, orbitals)
    energies = lax.map(group_energy, grouped).reshape(total_rows)
    biases = lax.dot_general(
        block_in.reshape(block_in.shape[0], occupied * orbitals),
        chol_rows,
        (((1,), (1,)), ((), ())),
        preferred_element_type=jnp.float32,
    )
    bias_mine, energy_cols = (
        lax.all_to_all(biases, "walk", split_axis=0, concat_axis=1, tiled=True),
        lax.all_to_all(energies[:, None], "walk", split_axis=0, concat_axis=1, tiled=True),
    )
    energy_mine = jnp.sum(energy_cols, axis=1)
    bias_near, energy_near = (
        padded(bias_mine, (("walk", 0),), old_slots),
        padded(energy_mine, (("walk", 0),), old_slots),
    )
    bias_rows = jnp.take(bias_near, chosen, axis=0)
    energy_slot = jnp.take(energy_near, chosen, axis=0)
    exchange_energy = jnp.where(is_live, energy_slot, 0.0)
    force_bias = jnp.where(is_live[:, None], bias_rows, 0.0)
    return (relocated, exchange_energy, force_bias)


def solution(mesh):
    return jax.shard_map(
        body,
        mesh=mesh,
        in_specs=(
            P(("rep", "walk"), None, None),
            P(("rep", "walk")),
            P("rep"),
            P("walk", None, None),
        ),
        out_specs=(P(("rep", "walk"), None, None), P(("rep", "walk")), P(("rep", "walk"), None)),
        check_vma=False,
    )
```

profile of v0, /device:TPU:0, one launch (start us, length us, event | category | flops | bytes accessed | tf_op | source)
XLA Modules:
  0.0 130.4 jit_solution(3880565610310121807)
XLA Ops:
  1.1 5.1 %collective-permute-start.1 = (bf16[1,64,384]{2,1,0:T(8,128)(2,1)}, bf16[1,64,384]{2,1,0:T(8,128)(2,1)S(1)}, u32[]{:S(2)}, u32[]{:S(2)}) collective-permute-start(bf16[1,64,384]{2,1,0:T(8,128)(2,1)} %param.6), channel_id=1, source_target_pairs={{1,0},{2,1},{3,2},{4,3},{5,4},{6,5},{7,6},{8,7},{9,8},{10,9},{11,1... | collective-permute-start | bytes 147464 | tf_op jit(solution)/shard_map/ppermute | solution.py:16
  6.2 21.7 %all_gather.3 = bf16[16,64,384]{2,1,0:T(8,128)(2,1)S(1)} all-gather(bf16[1,64,384]{2,1,0:T(8,128)(2,1)} %param.6), channel_id=1, replica_groups=mesh['rep'=2,'walk'=16] {'walk'}, dimensions={0}, use_global_device_ids=true | all-gather | bytes 835584 | tf_op jit(solution)/shard_map/all_gather | solution.py:54
  27.9 68.6 %while.10 = (s32[]{:T(128)}, f32[4,4]{1,0:T(4,128)S(1)}, bf16[4,4,64,384]{3,2,1,0:T(8,128)(2,1)S(1)}, bf16[32,64,384]{2,1,0:T(8,128)(2,1)}, s32[]{:T(128)}, /*index=5*/f32[]{:T(128)}, s32[]{:T(128)}) while((s32[]{:T(128)}, f32[4,4]{1,0:T(4,128)S(1)}, bf16[4,4,64,384]{3,2,1,0:T(8,128)(2,1)S(1)}, bf16[32,64,384]{2,1,0:T(8,128)(2,1)}, s32[]{:T(128)}, ...), condition=%wide.region_3.4_spmd, body=%wide.region_0.3_spmd.sunk | while | flops 403701760 | bytes 44107972 | solution.py:61
  30.4 4.3 %fusion.14 = f32[128,64,64]{2,1,0:T(8,128)} fusion(bf16[128,64,384]{2,1,0:T(8,128)(2,1)S(1)} %bitcast.33, bf16[128,64,384]{2,1,0:T(8,128)(2,1)S(1)} %bitcast.34), kind=kOutput, calls=%fused_computation.24.clone.1 | convolution fusion | flops 402653184 | bytes 14680064 | tf_op jit(solution)/shard_map/while/body/eval_jaxpr/dot_general | solution.py:50
  34.7 5.7 %copy.25 = f32[128,64,64]{1,2,0:T(8,128)} copy(f32[128,64,64]{2,1,0:T(8,128)} %fusion.14) | data formatting | bytes 4194304 | tf_op jit(solution)/shard_map/while/body/eval_jaxpr/dot_general | solution.py:50
  40.3 4.5 %fusion.15 = f32[128]{0:T(128)S(1)} fusion(f32[128,64,64]{2,1,0:T(8,128)} %fusion.14, f32[128,64,64]{1,2,0:T(8,128)} %copy.25), kind=kLoop, calls=%fused_computation.4.clone.1 | loop fusion | flops 1048448 | bytes 4194816 | tf_op jit(solution)/shard_map/while/body/eval_jaxpr/reduce_sum | solution.py:52
  47.6 4.3 %fusion.14 = f32[128,64,64]{2,1,0:T(8,128)} fusion(bf16[128,64,384]{2,1,0:T(8,128)(2,1)S(1)} %bitcast.33, bf16[128,64,384]{2,1,0:T(8,128)(2,1)S(1)} %bitcast.34), kind=kOutput, calls=%fused_computation.24.clone.1 | convolution fusion | flops 402653184 | bytes 14680064 | tf_op jit(solution)/shard_map/while/body/eval_jaxpr/dot_general | solution.py:50
  51.8 5.7 %copy.25 = f32[128,64,64]{1,2,0:T(8,128)} copy(f32[128,64,64]{2,1,0:T(8,128)} %fusion.14) | data formatting | bytes 4194304 | tf_op jit(solution)/shard_map/while/body/eval_jaxpr/dot_general | solution.py:50
  57.5 4.5 %fusion.15 = f32[128]{0:T(128)S(1)} fusion(f32[128,64,64]{2,1,0:T(8,128)} %fusion.14, f32[128,64,64]{1,2,0:T(8,128)} %copy.25), kind=kLoop, calls=%fused_computation.4.clone.1 | loop fusion | flops 1048448 | bytes 4194816 | tf_op jit(solution)/shard_map/while/body/eval_jaxpr/reduce_sum | solution.py:52
  64.7 4.3 %fusion.14 = f32[128,64,64]{2,1,0:T(8,128)} fusion(bf16[128,64,384]{2,1,0:T(8,128)(2,1)S(1)} %bitcast.33, bf16[128,64,384]{2,1,0:T(8,128)(2,1)S(1)} %bitcast.34), kind=kOutput, calls=%fused_computation.24.clone.1 | convolution fusion | flops 402653184 | bytes 14680064 | tf_op jit(solution)/shard_map/while/body/eval_jaxpr/dot_general | solution.py:50
  69.0 5.7 %copy.25 = f32[128,64,64]{1,2,0:T(8,128)} copy(f32[128,64,64]{2,1,0:T(8,128)} %fusion.14) | data formatting | bytes 4194304 | tf_op jit(solution)/shard_map/while/body/eval_jaxpr/dot_general | solution.py:50
  74.6 4.5 %fusion.15 = f32[128]{0:T(128)S(1)} fusion(f32[128,64,64]{2,1,0:T(8,128)} %fusion.14, f32[128,64,64]{1,2,0:T(8,128)} %copy.25), kind=kLoop, calls=%fused_computation.4.clone.1 | loop fusion | flops 1048448 | bytes 4194816 | tf_op jit(solution)/shard_map/while/body/eval_jaxpr/reduce_sum | solution.py:52
  81.8 4.3 %fusion.14 = f32[128,64,64]{2,1,0:T(8,128)} fusion(bf16[128,64,384]{2,1,0:T(8,128)(2,1)S(1)} %bitcast.33, bf16[128,64,384]{2,1,0:T(8,128)(2,1)S(1)} %bitcast.34), kind=kOutput, calls=%fused_computation.24.clone.1 | convolution fusion | flops 402653184 | bytes 14680064 | tf_op jit(solution)/shard_map/while/body/eval_jaxpr/dot_general | solution.py:50
  86.1 5.7 %copy.25 = f32[128,64,64]{1,2,0:T(8,128)} copy(f32[128,64,64]{2,1,0:T(8,128)} %fusion.14) | data formatting | bytes 4194304 | tf_op jit(solution)/shard_map/while/body/eval_jaxpr/dot_general | solution.py:50
  91.8 4.5 %fusion.15 = f32[128]{0:T(128)S(1)} fusion(f32[128,64,64]{2,1,0:T(8,128)} %fusion.14, f32[128,64,64]{1,2,0:T(8,128)} %copy.25), kind=kLoop, calls=%fused_computation.4.clone.1 | loop fusion | flops 1048448 | bytes 4194816 | tf_op jit(solution)/shard_map/while/body/eval_jaxpr/reduce_sum | solution.py:52
  97.2 3.5 %all-to-all-start = ((f32[16,1,1]{2,1,0:T(1,128)}), f32[16,1,1]{2,1,0:T(1,128)S(1)}, u32[]{:S(2)}, u32[]{:S(2)}) async-start(f32[16,1,1]{2,1,0:T(1,128)} %all_to_all.27), calls=%async_computation | async-start | bytes 16384 | tf_op jit(solution)/shard_map/all_to_all | solution.py:70
  100.7 3.7 %fusion.1 = f32[16,32,1]{1,0,2:T(8,128)} fusion(bf16[32,64,384]{2,1,0:T(8,128)(2,1)} %get-tuple-element.91, bf16[16,64,384]{2,1,0:T(8,128)(2,1)S(1)} %bitcast.36), kind=kOutput, calls=%fused_computation.7 | convolution fusion | flops 25165824 | bytes 2361344 | tf_op jit(solution)/shard_map/dot_general | solution.py:62
  105.7 1.3 all-to-all-done
  107.0 4.7 %all-to-all-start.1 = ((f32[16,1,32]{2,1,0:T(1,128)}), f32[16,1,32]{2,1,0:T(1,128)S(1)}, u32[]{:S(2)}, u32[]{:S(2)}) async-start(f32[16,1,32]{2,1,0:T(1,128)} %bitcast.10), calls=%async_computation.1 | async-start | bytes 16384 | tf_op jit(solution)/shard_map/all_to_all | solution.py:69
  112.7 4.0 %collective-permute-start.3 = (f32[1]{0:T(128)}, f32[1]{0:T(128)}, u32[]{:S(2)}, u32[]{:S(2)}) collective-permute-start(f32[1]{0:T(128)} %bitcast.7), channel_id=1, source_target_pairs={{1,0},{2,1},{3,2},{4,3},{5,4},{6,5},{7,6},{8,7},{9,8},{10,9},{11,1... | collective-permute-start | bytes 20 | tf_op jit(solution)/shard_map/ppermute | solution.py:16
  116.8 1.3 %collective-permute-done.2 = f32[1]{0:T(128)} collective-permute-done((f32[1]{0:T(128)}, f32[1]{0:T(128)}, u32[]{:S(2)}, u32[]{:S(2)}) %collective-permute-start.2) | collective-permute-done | bytes 36 | tf_op jit(solution)/shard_map/ppermute | solution.py:13
  118.2 2.0 %pad_maximum_fusion.2 = f32[3]{0:T(128)S(1)} fusion(f32[1]{0:T(128)} %collective-permute-done.3, f32[1]{0:T(128)} %bitcast.7, f32[1]{0:T(128)} %collective-permute-done.2), kind=kLoop, calls=%fused_computation.21 | loop fusion | flops 6 | bytes 24 | tf_op jit(solution)/shard_map/concatenate | solution.py:17
  122.1 4.4 %collective-permute-start.5 = (f32[1,512]{1,0:T(1,128)S(1)}, f32[1,512]{1,0:T(1,128)S(1)}, u32[]{:S(2)}, u32[]{:S(2)}) collective-permute-start(f32[1,512]{1,0:T(1,128)S(1)} %all_to_all.26), channel_id=1, source_target_pairs={{1,0},{2,1},{3,2},{4,3},{5,4},{6,5},{7,6},{8,7},{9,8},{10,9},{11,1... | collective-permute-start | bytes 6152 | tf_op jit(solution)/shard_map/ppermute | solution.py:16
  126.5 1.2 select_select_fusion.2
  (67 shorter events, 19.0 us)
Async XLA Ops:
  0.6 128.4 %collective-permute-start = (bf16[1,64,384]{2,1,0:T(8,128)(2,1)}, bf16[1,64,384]{2,1,0:T(8,128)(2,1)S(1)}, u32[]{:S(2)}, u32[]{:S(2)}) collective-permute-start(bf16[1,64,384]{2,1,0:T(8,128)(2,1)} %param.6), channel_id=1, source_target_pairs={{0,1},{1,2},{2,3},{3,4},{4,5},{5,6},{6,7},{7,8},{8,9},{9,10},{10,1... | collective-permute-start | bytes 147464 | tf_op jit(solution)/shard_map/ppermute | solution.py:13
  1.1 127.9 %collective-permute-start.1 = (bf16[1,64,384]{2,1,0:T(8,128)(2,1)}, bf16[1,64,384]{2,1,0:T(8,128)(2,1)S(1)}, u32[]{:S(2)}, u32[]{:S(2)}) collective-permute-start(bf16[1,64,384]{2,1,0:T(8,128)(2,1)} %param.6), channel_id=1, source_target_pairs={{1,0},{2,1},{3,2},{4,3},{5,4},{6,5},{7,6},{8,7},{9,8},{10,9},{11,1... | collective-permute-start | bytes 147464 | tf_op jit(solution)/shard_map/ppermute | solution.py:16
  27.9 76.5 %copy-start.3 = (s32[16]{0:T(128)S(1)}, s32[16]{0:T(128)}, u32[]{:S(2)}) copy-start(s32[16]{0:T(128)} %param.8) | copy-start | bytes 196
  27.9 77.1 %copy-start.2 = (s32[2]{0:T(128)S(1)}, s32[2]{0:T(128)}, u32[]{:S(2)}) copy-start(s32[2]{0:T(128)} %param.7) | copy-start | bytes 28
  27.9 101.2 %copy-start.1 = (bf16[1,64,384]{2,1,0:T(8,128)(2,1)S(1)}, bf16[1,64,384]{2,1,0:T(8,128)(2,1)}, u32[]{:S(2)}) copy-start(bf16[1,64,384]{2,1,0:T(8,128)(2,1)} %param.6) | copy-start | bytes 147460
  27.9 1.4 %copy-start = (bf16[32,64,384]{2,1,0:T(8,128)(2,1)S(1)}, bf16[32,64,384]{2,1,0:T(8,128)(2,1)}, u32[]{:S(2)}) copy-start(bf16[32,64,384]{2,1,0:T(8,128)(2,1)} %get-tuple-element.87) | copy-start | bytes 4718596 | tf_op jit(solution)/shard_map/while
  45.1 1.4 %copy-start = (bf16[32,64,384]{2,1,0:T(8,128)(2,1)S(1)}, bf16[32,64,384]{2,1,0:T(8,128)(2,1)}, u32[]{:S(2)}) copy-start(bf16[32,64,384]{2,1,0:T(8,128)(2,1)} %get-tuple-element.87) | copy-start | bytes 4718596 | tf_op jit(solution)/shard_map/while
  62.2 1.4 %copy-start = (bf16[32,64,384]{2,1,0:T(8,128)(2,1)S(1)}, bf16[32,64,384]{2,1,0:T(8,128)(2,1)}, u32[]{:S(2)}) copy-start(bf16[32,64,384]{2,1,0:T(8,128)(2,1)} %get-tuple-element.87) | copy-start | bytes 4718596 | tf_op jit(solution)/shard_map/while
  79.4 1.4 %copy-start = (bf16[32,64,384]{2,1,0:T(8,128)(2,1)S(1)}, bf16[32,64,384]{2,1,0:T(8,128)(2,1)}, u32[]{:S(2)}) copy-start(bf16[32,64,384]{2,1,0:T(8,128)(2,1)} %get-tuple-element.87) | copy-start | bytes 4718596 | tf_op jit(solution)/shard_map/while
  97.2 9.8 %all-to-all-start = ((f32[16,1,1]{2,1,0:T(1,128)}), f32[16,1,1]{2,1,0:T(1,128)S(1)}, u32[]{:S(2)}, u32[]{:S(2)}) async-start(f32[16,1,1]{2,1,0:T(1,128)} %all_to_all.27), calls=%async_computation | async-start | bytes 16384 | tf_op jit(solution)/shard_map/all_to_all | solution.py:70
  107.0 13.8 %all-to-all-start.1 = ((f32[16,1,32]{2,1,0:T(1,128)}), f32[16,1,32]{2,1,0:T(1,128)S(1)}, u32[]{:S(2)}, u32[]{:S(2)}) async-start(f32[16,1,32]{2,1,0:T(1,128)} %bitcast.10), calls=%async_computation.1 | async-start | bytes 16384 | tf_op jit(solution)/shard_map/all_to_all | solution.py:69
  112.3 5.7 %collective-permute-start.2 = (f32[1]{0:T(128)}, f32[1]{0:T(128)}, u32[]{:S(2)}, u32[]{:S(2)}) collective-permute-start(f32[1]{0:T(128)} %bitcast.7), channel_id=1, source_target_pairs={{0,1},{1,2},{2,3},{3,4},{4,5},{5,6},{6,7},{7,8},{8,9},{9,10},{10,1... | collective-permute-start | bytes 20 | tf_op jit(solution)/shard_map/ppermute | solution.py:13
  112.7 5.5 %collective-permute-start.3 = (f32[1]{0:T(128)}, f32[1]{0:T(128)}, u32[]{:S(2)}, u32[]{:S(2)}) collective-permute-start(f32[1]{0:T(128)} %bitcast.7), channel_id=1, source_target_pairs={{1,0},{2,1},{3,2},{4,3},{5,4},{6,5},{7,6},{8,7},{9,8},{10,9},{11,1... | collective-permute-start | bytes 20 | tf_op jit(solution)/shard_map/ppermute | solution.py:16
  122.1 5.7 %collective-permute-start.4 = (f32[1,512]{1,0:T(1,128)S(1)}, f32[1,512]{1,0:T(1,128)S(1)}, u32[]{:S(2)}, u32[]{:S(2)}) collective-permute-start(f32[1,512]{1,0:T(1,128)S(1)} %all_to_all.26), channel_id=1, source_target_pairs={{0,1},{1,2},{2,3},{3,4},{4,5},{5,6},{6,7},{7,8},{8,9},{9,10},{10,1... | collective-permute-start | bytes 6152 | tf_op jit(solution)/shard_map/ppermute | solution.py:13
  122.1 5.7 %collective-permute-start.5 = (f32[1,512]{1,0:T(1,128)S(1)}, f32[1,512]{1,0:T(1,128)S(1)}, u32[]{:S(2)}, u32[]{:S(2)}) collective-permute-start(f32[1,512]{1,0:T(1,128)S(1)} %all_to_all.26), channel_id=1, source_target_pairs={{1,0},{2,1},{3,2},{4,3},{5,4},{6,5},{7,6},{8,7},{9,8},{10,9},{11,1... | collective-permute-start | bytes 6152 | tf_op jit(solution)/shard_map/ppermute | solution.py:16
where the time goes:
time: 131 us; the launch traced here: 130 us
  local copies, waits for them, and re-layouts  36.5 us (28%)
  other arithmetic  25 us (19%)
  starting transfers between devices  22.6 us (17%)
  blocking collectives  21.7 us (17%)
  matrix products  20.8 us (16%)
  waiting for transfers between devices  2.86 us (2%)
    dot_general x4, local copies, waits for them, and re-layouts, group_energy(): lax.dot_general(stacked, spread, batch_dims, preferred_element_type=jnp.f...  22.6 us
    all_gather x1, blocking collectives, body(): block_in = lax.all_gather(greens, 'walk', axis=0, tiled=True)  21.7 us
    reduce_sum x8, other arithmetic, group_energy(): jnp.sum((forward * mirrored).reshape(members, -1), axis=1)  18.5 us
    dot_general x4, matrix products, group_energy(): lax.dot_general(stacked, spread, batch_dims, preferred_element_type=jnp.f...  17.1 us
    ppermute x3, starting transfers between devices, padded(): lax.ppermute(lax.slice_in_dim(block, 0, width, axis=dim), axis, backward)  13.5 us
    all_to_all x1, starting transfers between devices, body(): lax.all_to_all(biases, 'walk', split_axis=0, concat_axis=1, tiled=True)  4.71 us
    broadcast_in_dim x8, local copies, waits for them, and re-layouts, group_energy(): jnp.broadcast_to(group_in[:, None], (members, chol_dev, occupied, orbitals))  4.26 us
    broadcast_in_dim x4, local copies, waits for them, and re-layouts, group_energy(): jnp.broadcast_to(cholesky[None], (members, chol_dev, occupied, orbitals))  4.15 us
  transfers between devices with their start and end apart: 8, of which 4 were waited for; matrix products, arithmetic and copies ran while one was open for 61% of the time, Pallas kernels for 0%

commit v1 on v0

--- a/solution.py
+++ b/solution.py
@@ -67,7 +67,12 @@
     )
     bias_mine, energy_cols = (
         lax.all_to_all(biases, "walk", split_axis=0, concat_axis=1, tiled=True),
-        lax.all_to_all(energies[:, None], "walk", split_axis=0, concat_axis=1, tiled=True),
+        jnp.concatenate(
+            lax.all_to_all(
+                jnp.stack(jnp.split(energies[:, None], lax.axis_size("walk"), axis=0)), "walk", 0, 0
+            ),
+            axis=1,
+        ),
     )
     energy_mine = jnp.sum(energy_cols, axis=1)
     bias_near, energy_near = (

time: 131 us -> 150 us (1.15)
  local copies, waits for them, and re-layouts: 36.5 us -> 54.8 us
    unnamed x6 -> x21, local copies, waits for them, and re-layouts: 0.01 us -> 17 us
  transfers between devices with their start and end apart: 8 -> 8, of which waited for: 4 -> 4; matrix products, arithmetic and copies ran while one was open for 61% -> 66% of each run, Pallas kernels for 0% -> 0%
where the time goes in v1:
time: 150 us; the launch traced here: 149 us
  local copies, waits for them, and re-layouts  54.8 us (37%)
  other arithmetic  25 us (17%)
  starting transfers between devices  22.7 us (15%)
  blocking collectives  21.7 us (14%)
  matrix products  20.8 us (14%)
  waiting for transfers between devices  2.9 us (2%)
    dot_general x4, local copies, waits for them, and re-layouts, group_energy(): lax.dot_general(stacked, spread, batch_dims, preferred_element_type=jnp.f...  22.7 us
    all_gather x1, blocking collectives, body(): block_in = lax.all_gather(greens, 'walk', axis=0, tiled=True)  21.7 us
    reduce_sum x8, other arithmetic, group_energy(): jnp.sum((forward * mirrored).reshape(members, -1), axis=1)  18.5 us
    dot_general x4, matrix products, group_energy(): lax.dot_general(stacked, spread, batch_dims, preferred_element_type=jnp.f...  17.1 us
    unnamed x21, local copies, waits for them, and re-layouts  17 us
    ppermute x3, starting transfers between devices, padded(): lax.ppermute(lax.slice_in_dim(block, 0, width, axis=dim), axis, backward)  13.6 us
    all_to_all x1, starting transfers between devices, body(): lax.all_to_all(biases, 'walk', split_axis=0, concat_axis=1, tiled=True)  4.71 us
    broadcast_in_dim x8, local copies, waits for them, and re-layouts, group_energy(): jnp.broadcast_to(group_in[:, None], (members, chol_dev, occupied, orbitals))  4.26 us
  transfers between devices with their start and end apart: 8, of which 4 were waited for; matrix products, arithmetic and copies ran while one was open for 66% of the time, Pallas kernels for 0%

profile of v1, /device:TPU:0, one launch (start us, length us, event | category | flops | bytes accessed | tf_op | source)
XLA Modules:
  0.0 148.8 jit_solution(3029773397947720061)
XLA Ops:
  1.1 5.1 %collective-permute-start.1 = (bf16[1,64,384]{2,1,0:T(8,128)(2,1)}, bf16[1,64,384]{2,1,0:T(8,128)(2,1)S(1)}, u32[]{:S(2)}, u32[]{:S(2)}) collective-permute-start(bf16[1,64,384]{2,1,0:T(8,128)(2,1)} %param.6), channel_id=1, source_target_pairs={{1,0},{2,1},{3,2},{4,3},{5,4},{6,5},{7,6},{8,7},{9,8},{10,9},{11,1... | collective-permute-start | bytes 147464 | tf_op jit(solution)/shard_map/ppermute | solution.py:16
  6.2 21.7 %all_gather.3 = bf16[16,64,384]{2,1,0:T(8,128)(2,1)S(1)} all-gather(bf16[1,64,384]{2,1,0:T(8,128)(2,1)} %param.6), channel_id=1, replica_groups=mesh['rep'=2,'walk'=16] {'walk'}, dimensions={0}, use_global_device_ids=true | all-gather | bytes 835584 | tf_op jit(solution)/shard_map/all_gather | solution.py:54
  27.9 68.6 %while.10 = (s32[]{:T(128)}, f32[4,4]{1,0:T(4,128)S(1)}, bf16[4,4,64,384]{3,2,1,0:T(8,128)(2,1)S(1)}, bf16[32,64,384]{2,1,0:T(8,128)(2,1)}, s32[]{:T(128)}, /*index=5*/f32[]{:T(128)}, s32[]{:T(128)}) while((s32[]{:T(128)}, f32[4,4]{1,0:T(4,128)S(1)}, bf16[4,4,64,384]{3,2,1,0:T(8,128)(2,1)S(1)}, bf16[32,64,384]{2,1,0:T(8,128)(2,1)}, s32[]{:T(128)}, ...), condition=%wide.region_3.4_spmd, body=%wide.region_0.3_spmd.sunk | while | flops 403701760 | bytes 44107972 | solution.py:61
  30.4 4.3 %fusion.15 = f32[128,64,64]{2,1,0:T(8,128)} fusion(bf16[128,64,384]{2,1,0:T(8,128)(2,1)S(1)} %bitcast.79, bf16[128,64,384]{2,1,0:T(8,128)(2,1)S(1)} %bitcast.80), kind=kOutput, calls=%fused_computation.41.clone.1 | convolution fusion | flops 402653184 | bytes 14680064 | tf_op jit(solution)/shard_map/while/body/eval_jaxpr/dot_general | solution.py:50
  34.7 5.7 %copy.125 = f32[128,64,64]{1,2,0:T(8,128)} copy(f32[128,64,64]{2,1,0:T(8,128)} %fusion.15) | data formatting | bytes 4194304 | tf_op jit(solution)/shard_map/while/body/eval_jaxpr/dot_general | solution.py:50
  40.4 4.5 %fusion.16 = f32[128]{0:T(128)S(1)} fusion(f32[128,64,64]{2,1,0:T(8,128)} %fusion.15, f32[128,64,64]{1,2,0:T(8,128)} %copy.125), kind=kLoop, calls=%fused_computation.4.clone.1 | loop fusion | flops 1048448 | bytes 4194816 | tf_op jit(solution)/shard_map/while/body/eval_jaxpr/reduce_sum | solution.py:52
  47.6 4.3 %fusion.15 = f32[128,64,64]{2,1,0:T(8,128)} fusion(bf16[128,64,384]{2,1,0:T(8,128)(2,1)S(1)} %bitcast.79, bf16[128,64,384]{2,1,0:T(8,128)(2,1)S(1)} %bitcast.80), kind=kOutput, calls=%fused_computation.41.clone.1 | convolution fusion | flops 402653184 | bytes 14680064 | tf_op jit(solution)/shard_map/while/body/eval_jaxpr/dot_general | solution.py:50
  51.8 5.7 %copy.125 = f32[128,64,64]{1,2,0:T(8,128)} copy(f32[128,64,64]{2,1,0:T(8,128)} %fusion.15) | data formatting | bytes 4194304 | tf_op jit(solution)/shard_map/while/body/eval_jaxpr/dot_general | solution.py:50
  57.5 4.5 %fusion.16 = f32[128]{0:T(128)S(1)} fusion(f32[128,64,64]{2,1,0:T(8,128)} %fusion.15, f32[128,64,64]{1,2,0:T(8,128)} %copy.125), kind=kLoop, calls=%fused_computation.4.clone.1 | loop fusion | flops 1048448 | bytes 4194816 | tf_op jit(solution)/shard_map/while/body/eval_jaxpr/reduce_sum | solution.py:52
  64.7 4.3 %fusion.15 = f32[128,64,64]{2,1,0:T(8,128)} fusion(bf16[128,64,384]{2,1,0:T(8,128)(2,1)S(1)} %bitcast.79, bf16[128,64,384]{2,1,0:T(8,128)(2,1)S(1)} %bitcast.80), kind=kOutput, calls=%fused_computation.41.clone.1 | convolution fusion | flops 402653184 | bytes 14680064 | tf_op jit(solution)/shard_map/while/body/eval_jaxpr/dot_general | solution.py:50
  69.0 5.7 %copy.125 = f32[128,64,64]{1,2,0:T(8,128)} copy(f32[128,64,64]{2,1,0:T(8,128)} %fusion.15) | data formatting | bytes 4194304 | tf_op jit(solution)/shard_map/while/body/eval_jaxpr/dot_general | solution.py:50
  74.7 4.5 %fusion.16 = f32[128]{0:T(128)S(1)} fusion(f32[128,64,64]{2,1,0:T(8,128)} %fusion.15, f32[128,64,64]{1,2,0:T(8,128)} %copy.125), kind=kLoop, calls=%fused_computation.4.clone.1 | loop fusion | flops 1048448 | bytes 4194816 | tf_op jit(solution)/shard_map/while/body/eval_jaxpr/reduce_sum | solution.py:52
  81.9 4.3 %fusion.15 = f32[128,64,64]{2,1,0:T(8,128)} fusion(bf16[128,64,384]{2,1,0:T(8,128)(2,1)S(1)} %bitcast.79, bf16[128,64,384]{2,1,0:T(8,128)(2,1)S(1)} %bitcast.80), kind=kOutput, calls=%fused_computation.41.clone.1 | convolution fusion | flops 402653184 | bytes 14680064 | tf_op jit(solution)/shard_map/while/body/eval_jaxpr/dot_general | solution.py:50
  86.1 5.7 %copy.125 = f32[128,64,64]{1,2,0:T(8,128)} copy(f32[128,64,64]{2,1,0:T(8,128)} %fusion.15) | data formatting | bytes 4194304 | tf_op jit(solution)/shard_map/while/body/eval_jaxpr/dot_general | solution.py:50
  91.8 4.5 %fusion.16 = f32[128]{0:T(128)S(1)} fusion(f32[128,64,64]{2,1,0:T(8,128)} %fusion.15, f32[128,64,64]{1,2,0:T(8,128)} %copy.125), kind=kLoop, calls=%fused_computation.4.clone.1 | loop fusion | flops 1048448 | bytes 4194816 | tf_op jit(solution)/shard_map/while/body/eval_jaxpr/reduce_sum | solution.py:52
  109.7 1.2 constant_dynamic-update-slice_fusion.4
  115.5 3.5 %all-to-all-start = ((f32[16,1,1]{2,1,0:T(1,128)}), f32[16,1,1]{2,1,0:T(1,128)S(1)}, u32[]{:S(2)}, u32[]{:S(2)}) async-start(f32[16,1,1]{2,1,0:T(1,128)} %constant_dynamic-update-slice_fusion), calls=%async_computation | async-start | bytes 16384 | tf_op jit(solution)/shard_map/all_to_all | solution.py:71
  119.0 3.7 %fusion.1 = f32[16,32,1]{1,0,2:T(8,128)} fusion(bf16[32,64,384]{2,1,0:T(8,128)(2,1)} %get-tuple-element.107, bf16[16,64,384]{2,1,0:T(8,128)(2,1)S(1)} %bitcast.82), kind=kOutput, calls=%fused_computation.7 | convolution fusion | flops 25165824 | bytes 2361344 | tf_op jit(solution)/shard_map/dot_general | solution.py:62
  124.0 1.3 all-to-all-done
  125.3 4.7 %all-to-all-start.1 = ((f32[16,1,32]{2,1,0:T(1,128)}), f32[16,1,32]{2,1,0:T(1,128)S(1)}, u32[]{:S(2)}, u32[]{:S(2)}) async-start(f32[16,1,32]{2,1,0:T(1,128)} %bitcast.26), calls=%async_computation.1 | async-start | bytes 16384 | tf_op jit(solution)/shard_map/all_to_all | solution.py:69
  131.0 4.0 %collective-permute-start.3 = (f32[1]{0:T(128)}, f32[1]{0:T(128)}, u32[]{:S(2)}, u32[]{:S(2)}) collective-permute-start(f32[1]{0:T(128)} %bitcast.23), channel_id=1, source_target_pairs={{1,0},{2,1},{3,2},{4,3},{5,4},{6,5},{7,6},{8,7},{9,8},{10,9},{11,1... | collective-permute-start | bytes 20 | tf_op jit(solution)/shard_map/ppermute | solution.py:16
  135.1 1.5 collective-permute-done.2
  136.5 2.0 %pad_maximum_fusion.2 = f32[3]{0:T(128)S(1)} fusion(f32[1]{0:T(128)} %collective-permute-done.3, f32[1]{0:T(128)} %bitcast.23, f32[1]{0:T(128)} %collective-permute-done.2), kind=kLoop, calls=%fused_computation.37 | loop fusion | flops 6 | bytes 24 | tf_op jit(solution)/shard_map/concatenate | solution.py:17
  140.4 4.5 %collective-permute-start.5 = (f32[1,512]{1,0:T(1,128)S(1)}, f32[1,512]{1,0:T(1,128)S(1)}, u32[]{:S(2)}, u32[]{:S(2)}) collective-permute-start(f32[1,512]{1,0:T(1,128)S(1)} %all_to_all.18), channel_id=1, source_target_pairs={{1,0},{2,1},{3,2},{4,3},{5,4},{6,5},{7,6},{8,7},{9,8},{10,9},{11,1... | collective-permute-start | bytes 6152 | tf_op jit(solution)/shard_map/ppermute | solution.py:16
  (84 shorter events, 37.0 us)
Async XLA Ops:
  0.6 146.8 %collective-permute-start = (bf16[1,64,384]{2,1,0:T(8,128)(2,1)}, bf16[1,64,384]{2,1,0:T(8,128)(2,1)S(1)}, u32[]{:S(2)}, u32[]{:S(2)}) collective-permute-start(bf16[1,64,384]{2,1,0:T(8,128)(2,1)} %param.6), channel_id=1, source_target_pairs={{0,1},{1,2},{2,3},{3,4},{4,5},{5,6},{6,7},{7,8},{8,9},{9,10},{10,1... | collective-permute-start | bytes 147464 | tf_op jit(solution)/shard_map/ppermute | solution.py:13
  1.1 146.3 %collective-permute-start.1 = (bf16[1,64,384]{2,1,0:T(8,128)(2,1)}, bf16[1,64,384]{2,1,0:T(8,128)(2,1)S(1)}, u32[]{:S(2)}, u32[]{:S(2)}) collective-permute-start(bf16[1,64,384]{2,1,0:T(8,128)(2,1)} %param.6), channel_id=1, source_target_pairs={{1,0},{2,1},{3,2},{4,3},{5,4},{6,5},{7,6},{8,7},{9,8},{10,9},{11,1... | collective-permute-start | bytes 147464 | tf_op jit(solution)/shard_map/ppermute | solution.py:16
  27.9 94.8 %copy-start.3 = (s32[16]{0:T(128)S(1)}, s32[16]{0:T(128)}, u32[]{:S(2)}) copy-start(s32[16]{0:T(128)} %param.8) | copy-start | bytes 196
  27.9 95.4 %copy-start.2 = (s32[2]{0:T(128)S(1)}, s32[2]{0:T(128)}, u32[]{:S(2)}) copy-start(s32[2]{0:T(128)} %param.7) | copy-start | bytes 28
  27.9 119.5 %copy-start.1 = (bf16[1,64,384]{2,1,0:T(8,128)(2,1)S(1)}, bf16[1,64,384]{2,1,0:T(8,128)(2,1)}, u32[]{:S(2)}) copy-start(bf16[1,64,384]{2,1,0:T(8,128)(2,1)} %param.6) | copy-start | bytes 147460
  27.9 1.4 copy-start
  45.1 1.4 copy-start
  62.3 1.4 copy-start
  79.4 1.4 copy-start
  115.5 9.8 %all-to-all-start = ((f32[16,1,1]{2,1,0:T(1,128)}), f32[16,1,1]{2,1,0:T(1,128)S(1)}, u32[]{:S(2)}, u32[]{:S(2)}) async-start(f32[16,1,1]{2,1,0:T(1,128)} %constant_dynamic-update-slice_fusion), calls=%async_computation | async-start | bytes 16384 | tf_op jit(solution)/shard_map/all_to_all | solution.py:71
  125.3 13.9 %all-to-all-start.1 = ((f32[16,1,32]{2,1,0:T(1,128)}), f32[16,1,32]{2,1,0:T(1,128)S(1)}, u32[]{:S(2)}, u32[]{:S(2)}) async-start(f32[16,1,32]{2,1,0:T(1,128)} %bitcast.26), calls=%async_computation.1 | async-start | bytes 16384 | tf_op jit(solution)/shard_map/all_to_all | solution.py:69
  130.6 5.9 %collective-permute-start.2 = (f32[1]{0:T(128)}, f32[1]{0:T(128)}, u32[]{:S(2)}, u32[]{:S(2)}) collective-permute-start(f32[1]{0:T(128)} %bitcast.23), channel_id=1, source_target_pairs={{0,1},{1,2},{2,3},{3,4},{4,5},{5,6},{6,7},{7,8},{8,9},{9,10},{10,1... | collective-permute-start | bytes 20 | tf_op jit(solution)/shard_map/ppermute | solution.py:13
  131.0 5.5 %collective-permute-start.3 = (f32[1]{0:T(128)}, f32[1]{0:T(128)}, u32[]{:S(2)}, u32[]{:S(2)}) collective-permute-start(f32[1]{0:T(128)} %bitcast.23), channel_id=1, source_target_pairs={{1,0},{2,1},{3,2},{4,3},{5,4},{6,5},{7,6},{8,7},{9,8},{10,9},{11,1... | collective-permute-start | bytes 20 | tf_op jit(solution)/shard_map/ppermute | solution.py:16
  140.4 5.7 %collective-permute-start.4 = (f32[1,512]{1,0:T(1,128)S(1)}, f32[1,512]{1,0:T(1,128)S(1)}, u32[]{:S(2)}, u32[]{:S(2)}) collective-permute-start(f32[1,512]{1,0:T(1,128)S(1)} %all_to_all.18), channel_id=1, source_target_pairs={{0,1},{1,2},{2,3},{3,4},{4,5},{5,6},{6,7},{7,8},{8,9},{9,10},{10,1... | collective-permute-start | bytes 6152 | tf_op jit(solution)/shard_map/ppermute | solution.py:13
  140.4 5.8 %collective-permute-start.5 = (f32[1,512]{1,0:T(1,128)S(1)}, f32[1,512]{1,0:T(1,128)S(1)}, u32[]{:S(2)}, u32[]{:S(2)}) collective-permute-start(f32[1,512]{1,0:T(1,128)S(1)} %all_to_all.18), channel_id=1, source_target_pairs={{1,0},{2,1},{3,2},{4,3},{5,4},{6,5},{7,6},{8,7},{9,8},{10,9},{11,1... | collective-permute-start | bytes 6152 | tf_op jit(solution)/shard_map/ppermute | solution.py:16
